TPU v7x, 32 devices: a whole 2x2x4 slice. The times are simulated.
32 devices in a mesh: gx: 4 (over y, core), gy: 8 (over z, x).
Axes of the slice: x: 2, y: 2, z: 4, core: 2. Of those that a mesh axis runs over, the one named last changes fastest.
Arguments:
- source: float32 [256, 128, 128], P('gx', 'gy'), may hold values from -6 to 6
- diagonal: float32 [256, 128, 128], P('gx', 'gy'), may hold values from 6.05 to 7
- face_x: float32 [256, 128, 128], P('gx', 'gy'), may hold values from 0.1 to 1
- face_y: float32 [256, 128, 128], P('gx', 'gy'), may hold values from 0.1 to 1
- face_z: float32 [256, 128, 128], P('gx', 'gy'), may hold values from 0.1 to 1
- iterates: float32 [8, 256, 128, 128], P(None, 'gx', 'gy'), may hold values from -0.3 to 0.3
- labels: int32 [256, 128], P('gx', 'gy'), may hold values from 0 to 7
Outputs:
- new_iterates: float32 [8, 256, 128, 128], P(None, 'gx', 'gy')
- new_residual: float32 [256, 128, 128], P('gx', 'gy')
All inputs are finite; a program needn't handle non-finite values.
Results may differ from a plain program's by a relative error of at most 0.0003.
Values sent between devices are 32-bit elements; how exact they have to be, the bound alone decides.
No kernel may reach another device: no remote copies, remote signals or barrier semaphores. Data moves between devices by JAX's collectives and lax.ppermute only.
A program may use at most 128 MiB of HBM per device.

v0:
```python
import jax
import jax.numpy as jnp
from jax import lax
from jax.sharding import PartitionSpec as P

ENLARGE = 8
basis_shift = 6.5


def padded_2(block, sides, width):
    for axis, dim in sides:
        count = lax.axis_size(axis)
        forward = [(i, i + 1) for i in range(count - 1)]
        backward = [(target, source) for source, target in forward]
        low = lax.ppermute(
            lax.slice_in_dim(block, block.shape[dim] - width, None, axis=dim), axis, forward
        )
        high = lax.ppermute(lax.slice_in_dim(block, 0, width, axis=dim), axis, backward)
        block = jnp.concatenate([low, block, high], axis=dim)
    return block


def stencil(values, face_x, face_y, face_z, diagonal):
    centre = values[..., 1:-1, 1:-1, :]
    result = diagonal * centre
    result = (
        result
        - face_x[1:-1, 1:-1, :] * values[..., 2:, 1:-1, :]
        - face_x[:-2, 1:-1, :] * values[..., :-2, 1:-1, :]
    )
    result = (
        result
        - face_y[1:-1, 1:-1, :] * values[..., 1:-1, 2:, :]
        - face_y[1:-1, :-2, :] * values[..., 1:-1, :-2, :]
    )
    widths = [(0, 0)] * (centre.ndim - 1) + [(1, 1)]
    padded = jnp.pad(centre, widths)
    lower_face = jnp.pad(face_z[..., :-1], ((0, 0), (0, 0), (1, 0)))
    return result - face_z * padded[..., 2:] - lower_face * padded[..., :-2]


def finish(gram, project):
    highest = lax.Precision.HIGHEST
    lower = jnp.linalg.cholesky(gram)
    ident = jnp.eye(gram.shape[0], dtype=gram.dtype)
    inverse = lax.linalg.triangular_solve(lower, ident, left_side=True, lower=True)
    reduced = jnp.dot(jnp.dot(inverse, project, precision=highest), inverse.T, precision=highest)
    reduced = 0.5 * (reduced + reduced.T)
    target = jnp.dot(inverse, gram[:, :ENLARGE], precision=highest)
    factor = jnp.linalg.cholesky(reduced)
    middle = lax.linalg.triangular_solve(factor, target, left_side=True, lower=True)
    solved = lax.linalg.triangular_solve(
        factor, middle, left_side=True, lower=True, transpose_a=True
    )
    return jnp.dot(inverse.T, solved, precision=highest)


def shards(source, diagonal, face_x, face_y, face_z, iterates, labels):
    highest = lax.Precision.HIGHEST
    summed = jnp.sum(iterates, axis=0)
    columns = jnp.arange(ENLARGE, dtype=jnp.int32)
    near = (
        padded_2(summed, (("gx", 0), ("gy", 1)), 1),
        padded_2(face_x, (("gx", 0), ("gy", 1)), 1),
        padded_2(face_y, (("gx", 0), ("gy", 1)), 1),
    )
    near_sum, near_fx, near_fy = near
    residual = source - stencil(near_sum, near_fx, near_fy, face_z, diagonal)
    onehot = (labels[None] == columns[:, None, None]).astype(jnp.float32)
    blocks = residual[None] * onehot[..., None]
    blocks_wide = padded_2(blocks, (("gx", 1), ("gy", 2)), 1)
    applied = stencil(blocks_wide, near_fx, near_fy, face_z, diagonal)
    powered = applied - basis_shift * blocks
    powered_wide = padded_2(powered, (("gx", 1), ("gy", 2)), 1)
    second = stencil(powered_wide, near_fx, near_fy, face_z, diagonal)
    basis = jnp.concatenate([blocks, powered], axis=0)
    image = jnp.concatenate([applied, second], axis=0)
    gram_local = jnp.einsum("aijk,bijk->ab", basis, basis, precision=highest)
    project_local = jnp.einsum("aijk,bijk->ab", basis, image, precision=highest)
    gram = lax.psum(gram_local, ("gx", "gy"))
    project = lax.psum(project_local, ("gx", "gy"))
    coeffs = finish(gram, project)
    new_iterates = iterates + jnp.einsum("ab,aijk->bijk", coeffs, basis, precision=highest)
    carried = jnp.sum(coeffs, axis=1)
    new_residual = residual - jnp.einsum("a,aijk->ijk", carried, image, precision=highest)
    return (new_iterates, new_residual)


def solution(mesh):
    placed = (
        P("gx", "gy", None),
        P("gx", "gy", None),
        P("gx", "gy", None),
        P("gx", "gy", None),
        P("gx", "gy", None),
        P(None, "gx", "gy", None),
        P("gx", "gy"),
    )
    return jax.shard_map(
        shards,
        mesh=mesh,
        in_specs=placed,
        out_specs=(P(None, "gx", "gy", None), P("gx", "gy", None)),
        check_vma=False,
    )
```

profile of v0, /device:TPU:0, one launch (start us, length us, event | category | flops | bytes accessed | tf_op | source)
XLA Modules:
  0.0 177.3 jit_solution(15040397435094770270)
XLA Ops:
  0.7 2.7 %reduce_sum.18 = f32[64,16,128]{2,1,0:T(8,128)S(1)} reduce(f32[8,64,16,128]{3,2,1,0:T(8,128)} %param.13, f32[]{:T(128)} %constant.43.clone.1), dimensions={0}, to_apply=%region_0.0 | reduce | flops 917504 | bytes 4718596 | tf_op jit(solution)/shard_map/reduce_sum | solution.py:60
  4.7 3.0 %collective-permute-start.2 = (f32[1,16,128]{2,1,0:T(8,128)S(1)}, f32[1,16,128]{2,1,0:T(8,128)S(1)}, u32[]{:S(2)}, u32[]{:S(2)}) collective-permute-start(f32[1,16,128]{2,1,0:T(8,128)S(1)} %get-tuple-element.23), channel_id=1, source_target_pairs={{0,8},{8,16},{16,24},{1,9},{9,17},{17,25},{2,10},{10,18},{18,26},{... | collective-permute-start | bytes 24584 | tf_op jit(solution)/shard_map/ppermute | solution.py:15
  7.7 4.5 %collective-permute-start.4 = (f32[1,16,128]{2,1,0:T(8,128)S(1)}, f32[1,16,128]{2,1,0:T(8,128)S(1)}, u32[]{:S(2)}, u32[]{:S(2)}) collective-permute-start(f32[1,16,128]{2,1,0:T(8,128)S(1)} %get-tuple-element.22), channel_id=1, source_target_pairs={{0,8},{8,16},{16,24},{1,9},{9,17},{17,25},{2,10},{10,18},{18,26},{... | collective-permute-start | bytes 24584 | tf_op jit(solution)/shard_map/ppermute | solution.py:15
  13.6 3.0 %collective-permute-start.1 = (f32[1,16,128]{2,1,0:T(8,128)S(1)}, f32[1,16,128]{2,1,0:T(8,128)S(1)}, u32[]{:S(2)}, u32[]{:S(2)}) collective-permute-start(f32[1,16,128]{2,1,0:T(8,128)S(1)} %slice.156), channel_id=1, source_target_pairs={{0,8},{8,16},{16,24},{1,9},{9,17},{17,25},{2,10},{10,18},{18,26},{... | collective-permute-start | bytes 24584 | tf_op jit(solution)/shard_map/ppermute | solution.py:15
  18.1 4.5 %collective-permute-start.7 = (f32[66,1,128]{2,1,0:T(1,128)S(1)}, f32[66,1,128]{2,1,0:T(1,128)S(1)}, u32[]{:S(2)}, u32[]{:S(2)}) collective-permute-start(f32[66,1,128]{2,1,0:T(1,128)S(1)} %get-tuple-element.20), channel_id=1, source_target_pairs={{0,1},{1,2},{2,3},{3,4},{4,5},{5,6},{6,7},{8,9},{9,10},{10,11},{11... | collective-permute-start | bytes 101384 | tf_op jit(solution)/shard_map/ppermute | solution.py:15
  22.7 4.3 %collective-permute-start.6 = (f32[66,1,128]{2,1,0:T(1,128)S(1)}, f32[66,1,128]{2,1,0:T(1,128)S(1)}, u32[]{:S(2)}, u32[]{:S(2)}) collective-permute-start(f32[66,1,128]{2,1,0:T(1,128)S(1)} %slice.194), channel_id=1, source_target_pairs={{0,1},{1,2},{2,3},{3,4},{4,5},{5,6},{6,7},{8,9},{9,10},{10,11},{11... | collective-permute-start | bytes 101384 | tf_op jit(solution)/shard_map/ppermute | solution.py:15
  28.6 1.6 fusion.33
  32.8 3.0 %collective-permute-start.9 = (f32[8,1,16,128]{3,0,2,1:T(8,128)S(1)}, f32[8,1,16,128]{3,0,2,1:T(8,128)S(1)}, u32[]{:S(2)}, u32[]{:S(2)}) collective-permute-start(f32[8,1,16,128]{3,0,2,1:T(8,128)S(1)} %get-tuple-element.17), channel_id=1, source_target_pairs={{0,8},{8,16},{16,24},{1,9},{9,17},{17,25},{2,10},{10,18},{18,26},{... | collective-permute-start | bytes 196616 | tf_op jit(solution)/shard_map/ppermute | solution.py:15
  38.1 5.0 %collective-permute-start.11 = (f32[8,66,1,128]{3,0,2,1:T(8,128)S(1)}, f32[8,66,1,128]{3,0,2,1:T(8,128)S(1)}, u32[]{:S(2)}, u32[]{:S(2)}) collective-permute-start(f32[8,66,1,128]{3,0,2,1:T(8,128)S(1)} %get-tuple-element.14), channel_id=1, source_target_pairs={{0,1},{1,2},{2,3},{3,4},{4,5},{5,6},{6,7},{8,9},{9,10},{10,11},{11... | collective-permute-start | bytes 811016 | tf_op jit(solution)/shard_map/ppermute | solution.py:15
  43.4 4.0 %collective-permute-done.10 = f32[8,66,1,128]{3,0,2,1:T(8,128)S(1)} collective-permute-done((f32[8,66,1,128]{3,0,2,1:T(8,128)S(1)}, f32[8,66,1,128]{3,0,2,1:T(8,128)S(1)}, u32[]{:S(2)}, u32[]{:S(2)}) %collective-permute-start.10) | collective-permute-done | bytes 270368 | tf_op jit(solution)/shard_map/ppermute | solution.py:18
  47.4 7.2 %collective-permute-done.11 = f32[8,66,1,128]{3,0,2,1:T(8,128)S(1)} collective-permute-done((f32[8,66,1,128]{3,0,2,1:T(8,128)S(1)}, f32[8,66,1,128]{3,0,2,1:T(8,128)S(1)}, u32[]{:S(2)}, u32[]{:S(2)}) %collective-permute-start.11) | collective-permute-done | bytes 270368 | tf_op jit(solution)/shard_map/ppermute | solution.py:15
  54.6 7.5 %multiply_subtract_fusion = (f32[8,64,16,128]{3,0,2,1:T(8,128)S(1)}, f32[8,64,16,128]{3,0,2,1:T(8,128)S(1)}) fusion(f32[8,64,16]{0,2,1:T(8,128)S(1)} %fusion.43, f32[64,16,128]{2,1,0:T(8,128)S(1)} %get-tuple-element.9, f32[64,16,128]{2,1,0:T(8,128)S(1)} %pad.18, f32[8,64,16,128]{3,0,2,1:T(8,128)S(1)} %broadcast_multiply_fusion, ...), kind=kLoop, calls=%fused_computation.51 | loop fusion | flops 25165824 | bytes 17481728 | tf_op jit(solution)/shard_map/sub | solution.py:73
  63.4 3.0 %collective-permute-start.13 = (f32[8,1,16,128]{3,0,2,1:T(8,128)S(1)}, f32[8,1,16,128]{3,0,2,1:T(8,128)S(1)}, u32[]{:S(2)}, u32[]{:S(2)}) collective-permute-start(f32[8,1,16,128]{3,0,2,1:T(8,128)S(1)} %get-tuple-element.15), channel_id=1, source_target_pairs={{0,8},{8,16},{16,24},{1,9},{9,17},{17,25},{2,10},{10,18},{18,26},{... | collective-permute-start | bytes 196616 | tf_op jit(solution)/shard_map/ppermute | solution.py:15
  68.7 5.0 %collective-permute-start.15 = (f32[8,66,1,128]{3,0,2,1:T(8,128)S(1)}, f32[8,66,1,128]{3,0,2,1:T(8,128)S(1)}, u32[]{:S(2)}, u32[]{:S(2)}) collective-permute-start(f32[8,66,1,128]{3,0,2,1:T(8,128)S(1)} %get-tuple-element.12), channel_id=1, source_target_pairs={{0,1},{1,2},{2,3},{3,4},{4,5},{5,6},{6,7},{8,9},{9,10},{10,11},{11... | collective-permute-start | bytes 811016 | tf_op jit(solution)/shard_map/ppermute | solution.py:15
  73.7 11.2 %fusion.28 = f32[16,16]{0,1:T(8,128)S(1)} fusion(f32[8,64,16,128]{3,0,2,1:T(8,128)S(1)} %get-tuple-element.7, f32[8,64,16,128]{3,0,2,1:T(8,128)S(1)} %broadcast_multiply_fusion), kind=kOutput, calls=%fused_computation.55 | convolution fusion | flops 404750336 | bytes 8389632 | tf_op jit(solution)/shard_map/aijk,bijk->ab/dot_general | solution.py:78
  85.3 6.8 %fusion.10 = f32[8,64,16,128]{3,0,2,1:T(8,128)S(1)} fusion(f32[8,64,16,128]{3,0,2,1:T(8,128)S(1)} %get-tuple-element.7, f32[8,66,1,128]{3,0,2,1:T(8,128)S(1)} %collective-permute-done.15, f32[8,1,16,128]{3,0,2,1:T(8,128)S(1)} %collective-permute-done.12, f32[8,1,16,128]{3,0,2,1:T(8,128)S(1)} %collective-permute-done.13, ...), kind=kLoop, calls=%fused_computation.16 | loop fusion | flops 22020096 | bytes 12730368 | tf_op jit(solution)/shard_map/sub | solution.py:39
  92.1 1.9 %copy-done.5 = f32[8,64,16,128]{3,0,2,1:T(8,128)} copy-done((f32[8,64,16,128]{3,0,2,1:T(8,128)}, f32[8,64,16,128]{3,0,2,1:T(8,128)S(1)}, u32[]{:S(2)}) %copy-start.5) | copy-done | bytes 4194328
  94.1 10.4 %fusion.29 = f32[16,16]{1,0:T(8,128)S(1)} fusion(f32[8,64,16,128]{3,0,2,1:T(8,128)S(1)} %fusion.10, f32[8,64,16,128]{3,0,2,1:T(8,128)S(1)} %get-tuple-element.8, f32[8,64,16,128]{3,0,2,1:T(8,128)S(1)} %get-tuple-element.7, f32[8,64,16,128]{3,0,2,1:T(8,128)S(1)} %broadcast_multiply_fusion), kind=kOutput, calls=%fused_computation.56 | convolution fusion | flops 406847488 | bytes 16778240 | tf_op jit(solution)/shard_map/aijk,bijk->ab/dot_general | solution.py:79
  104.5 44.6 %all-reduce.4 = (f32[16,16]{0,1:T(8,128)S(1)}, f32[16,16]{1,0:T(8,128)S(1)}) all-reduce(f32[16,16]{0,1:T(8,128)S(1)} %fusion.28, f32[16,16]{1,0:T(8,128)S(1)} %fusion.29), channel_id=1, replica_groups=mesh['gx'=4,'gy'=8] {'gx','gy'}, use_global_device_ids=true, to_apply=%region_1.2 | all-reduce | flops 512 | bytes 4096 | tf_op jit(solution)/shard_map/psum | solution.py:80
  149.1 1.5 cholesky.44
  153.9 1.5 cholesky.55
  158.5 6.6 %fusion = f32[1,64,16,128]{3,0,2,1:T(1,128)S(1)} fusion(f32[8,64,16,128]{3,0,2,1:T(8,128)} %copy-done.5, f32[8,64,16,128]{3,0,2,1:T(8,128)} %copy-done.4, f32[16]{0:T(128)S(1)} %get-tuple-element.25), kind=kOutput, calls=%fused_computation.6 | convolution fusion | flops 27262976 | bytes 8912960 | tf_op jit(solution)/shard_map/a,aijk->ijk/dot_general | solution.py:85
  166.0 8.6 %copy_add_fusion = f32[8,64,16,128]{3,0,2,1:T(8,128)S(1)} fusion(f32[8,64,16,128]{3,2,1,0:T(8,128)} %param.13, f32[8,64,16,128]{3,0,2,1:T(8,128)S(1)} %copy-done.3, f32[8,64,16,128]{3,0,2,1:T(8,128)S(1)} %copy-done.1, f32[16,8]{0,1:T(8,128)S(1)} %get-tuple-element.26), kind=kOutput, calls=%fused_computation.50 | convolution fusion | flops 204472320 | bytes 16777728 | tf_op jit(solution)/shard_map/ab,aijk->bijk/dot_general | solution.py:83
  174.6 2.8 %copy.15 = f32[8,64,16,128]{3,2,1,0:T(8,128)} copy(f32[8,64,16,128]{3,0,2,1:T(8,128)S(1)} %copy_add_fusion) | data formatting | bytes 8388608
  (81 shorter events, 22.0 us)
Async XLA Ops:
  0.6 12.9 %copy-start.8 = (f32[64,16,128]{2,1,0:T(8,128)S(1)}, f32[64,16,128]{2,1,0:T(8,128)}, u32[]{:S(2)}) copy-start(f32[64,16,128]{2,1,0:T(8,128)} %param.10) | copy-start | bytes 1572868
  0.7 15.9 %copy-start.10 = (s32[64,16]{0,1:T(8,128)S(1)}, s32[64,16]{0,1:T(8,128)}, u32[]{:S(2)}) copy-start(s32[64,16]{0,1:T(8,128)} %param.14) | copy-start | bytes 12292
  0.7 28.0 %copy-start.6 = (f32[64,16,128]{2,1,0:T(8,128)S(1)}, f32[64,16,128]{2,1,0:T(8,128)}, u32[]{:S(2)}) copy-start(f32[64,16,128]{2,1,0:T(8,128)} %param.12) | copy-start | bytes 1572868
  0.7 28.0 %copy-start.9 = (f32[64,16,128]{2,1,0:T(8,128)S(1)}, f32[64,16,128]{2,1,0:T(8,128)}, u32[]{:S(2)}) copy-start(f32[64,16,128]{2,1,0:T(8,128)} %param.9) | copy-start | bytes 1572868
  3.4 13.3 %collective-permute-start = (f32[1,16,128]{2,1,0:T(8,128)S(1)}, f32[1,16,128]{2,1,0:T(8,128)S(1)}, u32[]{:S(2)}, u32[]{:S(2)}) collective-permute-start(f32[1,16,128]{2,1,0:T(8,128)S(1)} %get-tuple-element.24), channel_id=1, source_target_pairs={{8,0},{16,8},{24,16},{9,1},{17,9},{25,17},{10,2},{18,10},{26,18},{... | collective-permute-start | bytes 24584 | tf_op jit(solution)/shard_map/ppermute | solution.py:18
  4.7 12.0 %collective-permute-start.2 = (f32[1,16,128]{2,1,0:T(8,128)S(1)}, f32[1,16,128]{2,1,0:T(8,128)S(1)}, u32[]{:S(2)}, u32[]{:S(2)}) collective-permute-start(f32[1,16,128]{2,1,0:T(8,128)S(1)} %get-tuple-element.23), channel_id=1, source_target_pairs={{0,8},{8,16},{16,24},{1,9},{9,17},{17,25},{2,10},{10,18},{18,26},{... | collective-permute-start | bytes 24584 | tf_op jit(solution)/shard_map/ppermute | solution.py:15
  7.7 14.9 %collective-permute-start.4 = (f32[1,16,128]{2,1,0:T(8,128)S(1)}, f32[1,16,128]{2,1,0:T(8,128)S(1)}, u32[]{:S(2)}, u32[]{:S(2)}) collective-permute-start(f32[1,16,128]{2,1,0:T(8,128)S(1)} %get-tuple-element.22), channel_id=1, source_target_pairs={{0,8},{8,16},{16,24},{1,9},{9,17},{17,25},{2,10},{10,18},{18,26},{... | collective-permute-start | bytes 24584 | tf_op jit(solution)/shard_map/ppermute | solution.py:15
  12.2 10.4 %collective-permute-start.5 = (f32[1,16,128]{2,1,0:T(8,128)S(1)}, f32[1,16,128]{2,1,0:T(8,128)S(1)}, u32[]{:S(2)}, u32[]{:S(2)}) collective-permute-start(f32[1,16,128]{2,1,0:T(8,128)S(1)} %get-tuple-element.21), channel_id=1, source_target_pairs={{8,0},{16,8},{24,16},{9,1},{17,9},{25,17},{10,2},{18,10},{26,18},{... | collective-permute-start | bytes 24584 | tf_op jit(solution)/shard_map/ppermute | solution.py:18
  13.6 13.7 %collective-permute-start.1 = (f32[1,16,128]{2,1,0:T(8,128)S(1)}, f32[1,16,128]{2,1,0:T(8,128)S(1)}, u32[]{:S(2)}, u32[]{:S(2)}) collective-permute-start(f32[1,16,128]{2,1,0:T(8,128)S(1)} %slice.156), channel_id=1, source_target_pairs={{0,8},{8,16},{16,24},{1,9},{9,17},{17,25},{2,10},{10,18},{18,26},{... | collective-permute-start | bytes 24584 | tf_op jit(solution)/shard_map/ppermute | solution.py:15
  16.8 10.5 %collective-permute-start.3 = (f32[66,1,128]{2,1,0:T(1,128)S(1)}, f32[66,1,128]{2,1,0:T(1,128)S(1)}, u32[]{:S(2)}, u32[]{:S(2)}) collective-permute-start(f32[66,1,128]{2,1,0:T(1,128)S(1)} %get-tuple-element.19), channel_id=1, source_target_pairs={{1,0},{2,1},{3,2},{4,3},{5,4},{6,5},{7,6},{9,8},{10,9},{11,10},{12... | collective-permute-start | bytes 101384 | tf_op jit(solution)/shard_map/ppermute | solution.py:18
  18.1 9.2 %collective-permute-start.7 = (f32[66,1,128]{2,1,0:T(1,128)S(1)}, f32[66,1,128]{2,1,0:T(1,128)S(1)}, u32[]{:S(2)}, u32[]{:S(2)}) collective-permute-start(f32[66,1,128]{2,1,0:T(1,128)S(1)} %get-tuple-element.20), channel_id=1, source_target_pairs={{0,1},{1,2},{2,3},{3,4},{4,5},{5,6},{6,7},{8,9},{9,10},{10,11},{11... | collective-permute-start | bytes 101384 | tf_op jit(solution)/shard_map/ppermute | solution.py:15
  22.7 5.9 %collective-permute-start.6 = (f32[66,1,128]{2,1,0:T(1,128)S(1)}, f32[66,1,128]{2,1,0:T(1,128)S(1)}, u32[]{:S(2)}, u32[]{:S(2)}) collective-permute-start(f32[66,1,128]{2,1,0:T(1,128)S(1)} %slice.194), channel_id=1, source_target_pairs={{0,1},{1,2},{2,3},{3,4},{4,5},{5,6},{6,7},{8,9},{9,10},{10,11},{11... | collective-permute-start | bytes 101384 | tf_op jit(solution)/shard_map/ppermute | solution.py:15
  31.5 60.6 %copy-start = (f32[8,64,16,128]{3,0,2,1:T(8,128)}, f32[8,64,16,128]{3,0,2,1:T(8,128)S(1)}, u32[]{:S(2)}) copy-start(f32[8,64,16,128]{3,0,2,1:T(8,128)S(1)} %broadcast_multiply_fusion) | copy-start | bytes 12582916
  31.5 4.3 %collective-permute-start.8 = (f32[8,1,16,128]{3,0,2,1:T(8,128)S(1)}, f32[8,1,16,128]{3,0,2,1:T(8,128)S(1)}, u32[]{:S(2)}, u32[]{:S(2)}) collective-permute-start(f32[8,1,16,128]{3,0,2,1:T(8,128)S(1)} %get-tuple-element.18), channel_id=1, source_target_pairs={{8,0},{16,8},{24,16},{9,1},{17,9},{25,17},{10,2},{18,10},{26,18},{... | collective-permute-start | bytes 196616 | tf_op jit(solution)/shard_map/ppermute | solution.py:18
  32.8 3.9 %collective-permute-start.9 = (f32[8,1,16,128]{3,0,2,1:T(8,128)S(1)}, f32[8,1,16,128]{3,0,2,1:T(8,128)S(1)}, u32[]{:S(2)}, u32[]{:S(2)}) collective-permute-start(f32[8,1,16,128]{3,0,2,1:T(8,128)S(1)} %get-tuple-element.17), channel_id=1, source_target_pairs={{0,8},{8,16},{16,24},{1,9},{9,17},{17,25},{2,10},{10,18},{18,26},{... | collective-permute-start | bytes 196616 | tf_op jit(solution)/shard_map/ppermute | solution.py:15
  36.8 10.6 %collective-permute-start.10 = (f32[8,66,1,128]{3,0,2,1:T(8,128)S(1)}, f32[8,66,1,128]{3,0,2,1:T(8,128)S(1)}, u32[]{:S(2)}, u32[]{:S(2)}) collective-permute-start(f32[8,66,1,128]{3,0,2,1:T(8,128)S(1)} %get-tuple-element.13), channel_id=1, source_target_pairs={{1,0},{2,1},{3,2},{4,3},{5,4},{6,5},{7,6},{9,8},{10,9},{11,10},{12... | collective-permute-start | bytes 811016 | tf_op jit(solution)/shard_map/ppermute | solution.py:18
  38.1 16.6 %collective-permute-start.11 = (f32[8,66,1,128]{3,0,2,1:T(8,128)S(1)}, f32[8,66,1,128]{3,0,2,1:T(8,128)S(1)}, u32[]{:S(2)}, u32[]{:S(2)}) collective-permute-start(f32[8,66,1,128]{3,0,2,1:T(8,128)S(1)} %get-tuple-element.14), channel_id=1, source_target_pairs={{0,1},{1,2},{2,3},{3,4},{4,5},{5,6},{6,7},{8,9},{9,10},{10,11},{11... | collective-permute-start | bytes 811016 | tf_op jit(solution)/shard_map/ppermute | solution.py:15
  62.1 30.0 %copy-start.2 = (f32[8,64,16,128]{3,0,2,1:T(8,128)}, f32[8,64,16,128]{3,0,2,1:T(8,128)S(1)}, u32[]{:S(2)}) copy-start(f32[8,64,16,128]{3,0,2,1:T(8,128)S(1)} %get-tuple-element.7) | copy-start | bytes 12582916
  62.1 30.0 %copy-start.4 = (f32[8,64,16,128]{3,0,2,1:T(8,128)}, f32[8,64,16,128]{3,0,2,1:T(8,128)S(1)}, u32[]{:S(2)}) copy-start(f32[8,64,16,128]{3,0,2,1:T(8,128)S(1)} %get-tuple-element.8) | copy-start | bytes 12582916
  62.1 4.3 %collective-permute-start.12 = (f32[8,1,16,128]{3,0,2,1:T(8,128)S(1)}, f32[8,1,16,128]{3,0,2,1:T(8,128)S(1)}, u32[]{:S(2)}, u32[]{:S(2)}) collective-permute-start(f32[8,1,16,128]{3,0,2,1:T(8,128)S(1)} %get-tuple-element.16), channel_id=1, source_target_pairs={{8,0},{16,8},{24,16},{9,1},{17,9},{25,17},{10,2},{18,10},{26,18},{... | collective-permute-start | bytes 196616 | tf_op jit(solution)/shard_map/ppermute | solution.py:18
  63.4 3.9 %collective-permute-start.13 = (f32[8,1,16,128]{3,0,2,1:T(8,128)S(1)}, f32[8,1,16,128]{3,0,2,1:T(8,128)S(1)}, u32[]{:S(2)}, u32[]{:S(2)}) collective-permute-start(f32[8,1,16,128]{3,0,2,1:T(8,128)S(1)} %get-tuple-element.15), channel_id=1, source_target_pairs={{0,8},{8,16},{16,24},{1,9},{9,17},{17,25},{2,10},{10,18},{18,26},{... | collective-permute-start | bytes 196616 | tf_op jit(solution)/shard_map/ppermute | solution.py:15
  67.4 17.5 %collective-permute-start.14 = (f32[8,66,1,128]{3,0,2,1:T(8,128)S(1)}, f32[8,66,1,128]{3,0,2,1:T(8,128)S(1)}, u32[]{:S(2)}, u32[]{:S(2)}) collective-permute-start(f32[8,66,1,128]{3,0,2,1:T(8,128)S(1)} %get-tuple-element.11), channel_id=1, source_target_pairs={{1,0},{2,1},{3,2},{4,3},{5,4},{6,5},{7,6},{9,8},{10,9},{11,10},{12... | collective-permute-start | bytes 811016 | tf_op jit(solution)/shard_map/ppermute | solution.py:18
  68.7 16.6 %collective-permute-start.15 = (f32[8,66,1,128]{3,0,2,1:T(8,128)S(1)}, f32[8,66,1,128]{3,0,2,1:T(8,128)S(1)}, u32[]{:S(2)}, u32[]{:S(2)}) collective-permute-start(f32[8,66,1,128]{3,0,2,1:T(8,128)S(1)} %get-tuple-element.12), channel_id=1, source_target_pairs={{0,1},{1,2},{2,3},{3,4},{4,5},{5,6},{6,7},{8,9},{9,10},{10,11},{11... | collective-permute-start | bytes 811016 | tf_op jit(solution)/shard_map/ppermute | solution.py:15
  158.5 7.5 %copy-start.1 = (f32[8,64,16,128]{3,0,2,1:T(8,128)S(1)}, f32[8,64,16,128]{3,0,2,1:T(8,128)}, u32[]{:S(2)}) copy-start(f32[8,64,16,128]{3,0,2,1:T(8,128)} %copy-done) | copy-start | bytes 12582916
  (3 other events, 16.5 us)
where the time goes:
time: 178 us; the launch traced here: 177 us
  starting transfers between devices  44.6 us (25%)
  blocking collectives  44.6 us (25%)
  matrix products  37.9 us (21%)
  other arithmetic  29 us (16%)
  waiting for transfers between devices  14.8 us (8%)
  local copies, waits for them, and re-layouts  5.36 us (3%)
    psum x1, blocking collectives, shards(): gram = lax.psum(gram_local, ('gx', 'gy'))  44.6 us
    ppermute x9, starting transfers between devices, padded_2(): lax.ppermute(lax.slice_in_dim(block, block.shape[dim] - width, None, axis...  35.5 us
    dot_general x1, matrix products, shards(): gram_local = jnp.einsum('aijk,bijk->ab', basis, basis, precision=highest)  11.2 us
    ppermute x9, waiting for transfers between devices, padded_2(): lax.ppermute(lax.slice_in_dim(block, block.shape[dim] - width, None, axis...  10.7 us
    dot_general x1, matrix products, shards(): project_local = jnp.einsum('aijk,bijk->ab', basis, image, precision=highest)  10.4 us
    ppermute x7, starting transfers between devices, padded_2(): lax.ppermute(lax.slice_in_dim(block, 0, width, axis=dim), axis, backward)  9.04 us
    dot_general x1, matrix products, shards(): jnp.einsum('ab,aijk->bijk', coeffs, basis, precision=highest)  8.56 us
    sub x1, other arithmetic, shards(): powered = applied - basis_shift * blocks  7.45 us
  transfers between devices with their start and end apart: 16, of which 6 were waited for; matrix products, arithmetic and copies ran while one was open for 7% of the time, Pallas kernels for 0%

commit v1 on v0

--- a/solution.py
+++ b/solution.py
@@ -77,7 +77,7 @@
     image = jnp.concatenate([applied, second], axis=0)
     gram_local = jnp.einsum("aijk,bijk->ab", basis, basis, precision=highest)
     project_local = jnp.einsum("aijk,bijk->ab", basis, image, precision=highest)
-    gram = lax.psum(gram_local, ("gx", "gy"))
+    gram = jnp.sum(lax.all_gather(gram_local, ("gx", "gy")), axis=0)
     project = lax.psum(project_local, ("gx", "gy"))
     coeffs = finish(gram, project)
     new_iterates = iterates + jnp.einsum("ab,aijk->bijk", coeffs, basis, precision=highest)

time: 178 us -> 248 us (1.39)
  blocking collectives: 44.6 us -> 108 us
  other arithmetic: 29 us -> 32.3 us
    all_gather x0 -> x1, blocking collectives: none -> 67.5 us  [shards(): gram = jnp.sum(lax.all_gather(gram_local, ('gx', 'gy')), axis=0)]
    psum x1, blocking collectives: 44.6 us -> 40.4 us  [shards(): project = lax.psum(project_local, ('gx', 'gy'))]
  transfers between devices with their start and end apart: 16 -> 16, of which waited for: 6 -> 6; matrix products, arithmetic and copies ran while one was open for 7% -> 2% of each run, Pallas kernels for 0% -> 0%
where the time goes in v1:
time: 248 us; the launch traced here: 247 us
  blocking collectives  108 us (44%)
  starting transfers between devices  44.4 us (18%)
  matrix products  38.1 us (15%)
  other arithmetic  32.3 us (13%)
  waiting for transfers between devices  17.1 us (7%)
  local copies, waits for them, and re-layouts  6.09 us (2%)
    all_gather x1, blocking collectives, shards(): gram = jnp.sum(lax.all_gather(gram_local, ('gx', 'gy')), axis=0)  67.5 us
    psum x1, blocking collectives, shards(): project = lax.psum(project_local, ('gx', 'gy'))  40.4 us
    ppermute x9, starting transfers between devices, padded_2(): lax.ppermute(lax.slice_in_dim(block, block.shape[dim] - width, None, axis...  35.1 us
    dot_general x1, matrix products, shards(): gram_local = jnp.einsum('aijk,bijk->ab', basis, basis, precision=highest)  11.4 us
    ppermute x9, waiting for transfers between devices, padded_2(): lax.ppermute(lax.slice_in_dim(block, block.shape[dim] - width, None, axis...  10.9 us
    dot_general x1, matrix products, shards(): project_local = jnp.einsum('aijk,bijk->ab', basis, image, precision=highest)  10.4 us
    ppermute x7, starting transfers between devices, padded_2(): lax.ppermute(lax.slice_in_dim(block, 0, width, axis=dim), axis, backward)  9.32 us
    dot_general x1, matrix products, shards(): jnp.einsum('ab,aijk->bijk', coeffs, basis, precision=highest)  8.56 us
  transfers between devices with their start and end apart: 16, of which 6 were waited for; matrix products, arithmetic and copies ran while one was open for 2% of the time, Pallas kernels for 0%

profile of v1, /device:TPU:0, one launch (start us, length us, event | category | flops | bytes accessed | tf_op | source)
XLA Modules:
  0.0 247.0 jit_solution(3787354743446300611)
XLA Ops:
  0.7 2.7 %reduce_sum.27 = f32[64,16,128]{2,1,0:T(8,128)S(1)} reduce(f32[8,64,16,128]{3,2,1,0:T(8,128)} %param.13, f32[]{:T(128)} %constant.43.clone.1), dimensions={0}, to_apply=%region_0.0 | reduce | flops 917504 | bytes 4718596 | tf_op jit(solution)/shard_map/reduce_sum | solution.py:60
  4.7 3.0 %collective-permute-start.2 = (f32[1,16,128]{2,1,0:T(8,128)S(1)}, f32[1,16,128]{2,1,0:T(8,128)S(1)}, u32[]{:S(2)}, u32[]{:S(2)}) collective-permute-start(f32[1,16,128]{2,1,0:T(8,128)S(1)} %get-tuple-element.23), channel_id=1, source_target_pairs={{0,8},{8,16},{16,24},{1,9},{9,17},{17,25},{2,10},{10,18},{18,26},{... | collective-permute-start | bytes 24584 | tf_op jit(solution)/shard_map/ppermute | solution.py:15
  7.7 4.5 %collective-permute-start.4 = (f32[1,16,128]{2,1,0:T(8,128)S(1)}, f32[1,16,128]{2,1,0:T(8,128)S(1)}, u32[]{:S(2)}, u32[]{:S(2)}) collective-permute-start(f32[1,16,128]{2,1,0:T(8,128)S(1)} %get-tuple-element.22), channel_id=1, source_target_pairs={{0,8},{8,16},{16,24},{1,9},{9,17},{17,25},{2,10},{10,18},{18,26},{... | collective-permute-start | bytes 24584 | tf_op jit(solution)/shard_map/ppermute | solution.py:15
  13.6 3.0 %collective-permute-start.1 = (f32[1,16,128]{2,1,0:T(8,128)S(1)}, f32[1,16,128]{2,1,0:T(8,128)S(1)}, u32[]{:S(2)}, u32[]{:S(2)}) collective-permute-start(f32[1,16,128]{2,1,0:T(8,128)S(1)} %slice.156), channel_id=1, source_target_pairs={{0,8},{8,16},{16,24},{1,9},{9,17},{17,25},{2,10},{10,18},{18,26},{... | collective-permute-start | bytes 24584 | tf_op jit(solution)/shard_map/ppermute | solution.py:15
  18.1 4.5 %collective-permute-start.7 = (f32[66,1,128]{2,1,0:T(1,128)S(1)}, f32[66,1,128]{2,1,0:T(1,128)S(1)}, u32[]{:S(2)}, u32[]{:S(2)}) collective-permute-start(f32[66,1,128]{2,1,0:T(1,128)S(1)} %get-tuple-element.20), channel_id=1, source_target_pairs={{0,1},{1,2},{2,3},{3,4},{4,5},{5,6},{6,7},{8,9},{9,10},{10,11},{11... | collective-permute-start | bytes 101384 | tf_op jit(solution)/shard_map/ppermute | solution.py:15
  22.7 4.3 %collective-permute-start.6 = (f32[66,1,128]{2,1,0:T(1,128)S(1)}, f32[66,1,128]{2,1,0:T(1,128)S(1)}, u32[]{:S(2)}, u32[]{:S(2)}) collective-permute-start(f32[66,1,128]{2,1,0:T(1,128)S(1)} %slice.194), channel_id=1, source_target_pairs={{0,1},{1,2},{2,3},{3,4},{4,5},{5,6},{6,7},{8,9},{9,10},{10,11},{11... | collective-permute-start | bytes 101384 | tf_op jit(solution)/shard_map/ppermute | solution.py:15
  28.6 1.6 fusion.33
  33.0 3.0 %collective-permute-start.9 = (f32[8,1,16,128]{3,0,2,1:T(8,128)S(1)}, f32[8,1,16,128]{3,0,2,1:T(8,128)S(1)}, u32[]{:S(2)}, u32[]{:S(2)}) collective-permute-start(f32[8,1,16,128]{3,0,2,1:T(8,128)S(1)} %get-tuple-element.17), channel_id=1, source_target_pairs={{0,8},{8,16},{16,24},{1,9},{9,17},{17,25},{2,10},{10,18},{18,26},{... | collective-permute-start | bytes 196616 | tf_op jit(solution)/shard_map/ppermute | solution.py:15
  38.2 5.0 %collective-permute-start.11 = (f32[8,66,1,128]{3,0,2,1:T(8,128)S(1)}, f32[8,66,1,128]{3,0,2,1:T(8,128)S(1)}, u32[]{:S(2)}, u32[]{:S(2)}) collective-permute-start(f32[8,66,1,128]{3,0,2,1:T(8,128)S(1)} %get-tuple-element.14), channel_id=1, source_target_pairs={{0,1},{1,2},{2,3},{3,4},{4,5},{5,6},{6,7},{8,9},{9,10},{10,11},{11... | collective-permute-start | bytes 811016 | tf_op jit(solution)/shard_map/ppermute | solution.py:15
  43.5 4.0 %collective-permute-done.10 = f32[8,66,1,128]{3,0,2,1:T(8,128)S(1)} collective-permute-done((f32[8,66,1,128]{3,0,2,1:T(8,128)S(1)}, f32[8,66,1,128]{3,0,2,1:T(8,128)S(1)}, u32[]{:S(2)}, u32[]{:S(2)}) %collective-permute-start.10) | collective-permute-done | bytes 270368 | tf_op jit(solution)/shard_map/ppermute | solution.py:18
  47.6 7.2 %collective-permute-done.11 = f32[8,66,1,128]{3,0,2,1:T(8,128)S(1)} collective-permute-done((f32[8,66,1,128]{3,0,2,1:T(8,128)S(1)}, f32[8,66,1,128]{3,0,2,1:T(8,128)S(1)}, u32[]{:S(2)}, u32[]{:S(2)}) %collective-permute-start.11) | collective-permute-done | bytes 270368 | tf_op jit(solution)/shard_map/ppermute | solution.py:15
  54.8 8.3 %multiply_subtract_fusion = (f32[8,64,16,128]{3,0,2,1:T(8,128)S(1)}, f32[8,64,16,128]{3,0,2,1:T(8,128)}) fusion(f32[8,64,16]{0,2,1:T(8,128)S(1)} %fusion.43, f32[64,16,128]{2,1,0:T(8,128)S(1)} %get-tuple-element.9, f32[64,16,128]{2,1,0:T(8,128)S(1)} %pad.18, f32[8,64,16,128]{3,0,2,1:T(8,128)S(1)} %broadcast_multiply_fusion, f32[64,16,128]{2,1,0:T(8,128)S(1)} %copy-done.8, ...), kind=kLoop, calls=%fused_computation.51 | loop fusion | flops 25165824 | bytes 17481728 | tf_op jit(solution)/shard_map/sub | solution.py:73
  63.8 11.4 %fusion.28 = f32[16,16]{1,0:T(8,128)S(1)} fusion(f32[8,64,16,128]{3,0,2,1:T(8,128)S(1)} %get-tuple-element.7, f32[8,64,16,128]{3,0,2,1:T(8,128)S(1)} %broadcast_multiply_fusion), kind=kOutput, calls=%fused_computation.55 | convolution fusion | flops 404750336 | bytes 8389632 | tf_op jit(solution)/shard_map/aijk,bijk->ab/dot_general | solution.py:78
  76.5 3.0 %collective-permute-start.13 = (f32[8,1,16,128]{3,0,2,1:T(8,128)}, f32[8,1,16,128]{3,0,2,1:T(8,128)S(1)}, u32[]{:S(2)}, u32[]{:S(2)}) collective-permute-start(f32[8,1,16,128]{3,0,2,1:T(8,128)} %get-tuple-element.15), channel_id=1, source_target_pairs={{0,8},{8,16},{16,24},{1,9},{9,17},{17,25},{2,10},{10,18},{18,26},{... | collective-permute-start | bytes 196616 | tf_op jit(solution)/shard_map/ppermute | solution.py:15
  79.6 67.5 %all-gather = f32[512,16]{1,0:T(8,128)S(1)} all-gather(f32[16,16]{1,0:T(8,128)S(1)} %fusion.28), channel_id=2, replica_groups=mesh['gx'=4,'gy'=8] {'gx','gy'}, dimensions={0}, use_global_device_ids=true | all-gather | bytes 33792 | tf_op jit(solution)/shard_map/all_gather | solution.py:80
  154.0 4.6 %collective-permute-start.15 = (f32[8,66,1,128]{3,0,2,1:T(8,128)S(1)}, f32[8,66,1,128]{3,0,2,1:T(8,128)S(1)}, u32[]{:S(2)}, u32[]{:S(2)}) collective-permute-start(f32[8,66,1,128]{3,0,2,1:T(8,128)S(1)} %get-tuple-element.12), channel_id=1, source_target_pairs={{0,1},{1,2},{2,3},{3,4},{4,5},{5,6},{6,7},{8,9},{9,10},{10,11},{11... | collective-permute-start | bytes 811016 | tf_op jit(solution)/shard_map/ppermute | solution.py:15
  159.0 2.1 collective-permute-done.14
  162.6 7.9 %fusion.10 = f32[8,64,16,128]{3,0,2,1:T(8,128)S(1)} fusion(f32[8,64,16,128]{3,0,2,1:T(8,128)S(1)} %copy-done.4, f32[8,66,1,128]{3,0,2,1:T(8,128)S(1)} %collective-permute-done.15, f32[8,1,16,128]{3,0,2,1:T(8,128)S(1)} %collective-permute-done.12, f32[8,1,16,128]{3,0,2,1:T(8,128)S(1)} %collective-permute-done.13, ...), kind=kLoop, calls=%fused_computation.16 | loop fusion | flops 22020096 | bytes 12730368 | tf_op jit(solution)/shard_map/sub | solution.py:39
  170.4 2.0 copy-done.7
  172.4 10.4 %fusion.29 = f32[16,16]{1,0:T(8,128)S(1)} fusion(f32[8,64,16,128]{3,0,2,1:T(8,128)S(1)} %fusion.10, f32[8,64,16,128]{3,0,2,1:T(8,128)S(1)} %copy-done.6, f32[8,64,16,128]{3,0,2,1:T(8,128)S(1)} %copy-done.4, f32[8,64,16,128]{3,0,2,1:T(8,128)S(1)} %copy-done.1), kind=kOutput, calls=%fused_computation.56 | convolution fusion | flops 406847488 | bytes 16778240 | tf_op jit(solution)/shard_map/aijk,bijk->ab/dot_general | solution.py:79
  182.8 40.4 %psum.7 = f32[16,16]{1,0:T(8,128)S(1)} all-reduce(f32[16,16]{1,0:T(8,128)S(1)} %fusion.29), channel_id=1, replica_groups=mesh['gx'=4,'gy'=8] {'gx','gy'}, use_global_device_ids=true, to_apply=%region_4.6 | all-reduce | flops 256 | bytes 2048 | tf_op jit(solution)/shard_map/psum | solution.py:81
  228.2 6.6 %fusion = f32[1,64,16,128]{3,0,2,1:T(1,128)S(1)} fusion(f32[8,64,16,128]{3,0,2,1:T(8,128)} %copy-done.7, f32[8,64,16,128]{3,0,2,1:T(8,128)} %get-tuple-element.8, f32[16]{0:T(128)S(1)} %get-tuple-element.25), kind=kOutput, calls=%fused_computation.6 | convolution fusion | flops 27262976 | bytes 8912960 | tf_op jit(solution)/shard_map/a,aijk->ijk/dot_general | solution.py:85
  235.7 8.6 %copy_add_fusion = f32[8,64,16,128]{3,0,2,1:T(8,128)S(1)} fusion(f32[8,64,16,128]{3,2,1,0:T(8,128)} %param.13, f32[8,64,16,128]{3,0,2,1:T(8,128)S(1)} %copy-done.5, f32[8,64,16,128]{3,0,2,1:T(8,128)S(1)} %copy-done.2, f32[16,8]{0,1:T(8,128)S(1)} %get-tuple-element.26), kind=kOutput, calls=%fused_computation.50 | convolution fusion | flops 204472320 | bytes 16777728 | tf_op jit(solution)/shard_map/ab,aijk->bijk/dot_general | solution.py:83
  244.2 2.8 %copy.20 = f32[8,64,16,128]{3,2,1,0:T(8,128)} copy(f32[8,64,16,128]{3,0,2,1:T(8,128)S(1)} %copy_add_fusion) | data formatting | bytes 8388608
  (93 shorter events, 27.4 us)
Async XLA Ops:
  0.7 16.0 %copy-start.15 = (s32[64,16]{0,1:T(8,128)S(1)}, s32[64,16]{0,1:T(8,128)}, u32[]{:S(2)}) copy-start(s32[64,16]{0,1:T(8,128)} %param.14) | copy-start | bytes 12292
  0.7 28.0 %copy-start.8 = (f32[64,16,128]{2,1,0:T(8,128)S(1)}, f32[64,16,128]{2,1,0:T(8,128)}, u32[]{:S(2)}) copy-start(f32[64,16,128]{2,1,0:T(8,128)} %param.12) | copy-start | bytes 1572868
  0.7 28.0 %copy-start.11 = (f32[64,16,128]{2,1,0:T(8,128)S(1)}, f32[64,16,128]{2,1,0:T(8,128)}, u32[]{:S(2)}) copy-start(f32[64,16,128]{2,1,0:T(8,128)} %param.9) | copy-start | bytes 1572868
  3.4 13.3 %collective-permute-start = (f32[1,16,128]{2,1,0:T(8,128)S(1)}, f32[1,16,128]{2,1,0:T(8,128)S(1)}, u32[]{:S(2)}, u32[]{:S(2)}) collective-permute-start(f32[1,16,128]{2,1,0:T(8,128)S(1)} %get-tuple-element.24), channel_id=1, source_target_pairs={{8,0},{16,8},{24,16},{9,1},{17,9},{25,17},{10,2},{18,10},{26,18},{... | collective-permute-start | bytes 24584 | tf_op jit(solution)/shard_map/ppermute | solution.py:18
  4.7 12.0 %collective-permute-start.2 = (f32[1,16,128]{2,1,0:T(8,128)S(1)}, f32[1,16,128]{2,1,0:T(8,128)S(1)}, u32[]{:S(2)}, u32[]{:S(2)}) collective-permute-start(f32[1,16,128]{2,1,0:T(8,128)S(1)} %get-tuple-element.23), channel_id=1, source_target_pairs={{0,8},{8,16},{16,24},{1,9},{9,17},{17,25},{2,10},{10,18},{18,26},{... | collective-permute-start | bytes 24584 | tf_op jit(solution)/shard_map/ppermute | solution.py:15
  7.7 14.9 %collective-permute-start.4 = (f32[1,16,128]{2,1,0:T(8,128)S(1)}, f32[1,16,128]{2,1,0:T(8,128)S(1)}, u32[]{:S(2)}, u32[]{:S(2)}) collective-permute-start(f32[1,16,128]{2,1,0:T(8,128)S(1)} %get-tuple-element.22), channel_id=1, source_target_pairs={{0,8},{8,16},{16,24},{1,9},{9,17},{17,25},{2,10},{10,18},{18,26},{... | collective-permute-start | bytes 24584 | tf_op jit(solution)/shard_map/ppermute | solution.py:15
  12.2 10.4 %collective-permute-start.5 = (f32[1,16,128]{2,1,0:T(8,128)S(1)}, f32[1,16,128]{2,1,0:T(8,128)S(1)}, u32[]{:S(2)}, u32[]{:S(2)}) collective-permute-start(f32[1,16,128]{2,1,0:T(8,128)S(1)} %get-tuple-element.21), channel_id=1, source_target_pairs={{8,0},{16,8},{24,16},{9,1},{17,9},{25,17},{10,2},{18,10},{26,18},{... | collective-permute-start | bytes 24584 | tf_op jit(solution)/shard_map/ppermute | solution.py:18
  13.6 13.7 %collective-permute-start.1 = (f32[1,16,128]{2,1,0:T(8,128)S(1)}, f32[1,16,128]{2,1,0:T(8,128)S(1)}, u32[]{:S(2)}, u32[]{:S(2)}) collective-permute-start(f32[1,16,128]{2,1,0:T(8,128)S(1)} %slice.156), channel_id=1, source_target_pairs={{0,8},{8,16},{16,24},{1,9},{9,17},{17,25},{2,10},{10,18},{18,26},{... | collective-permute-start | bytes 24584 | tf_op jit(solution)/shard_map/ppermute | solution.py:15
  16.8 10.5 %collective-permute-start.3 = (f32[66,1,128]{2,1,0:T(1,128)S(1)}, f32[66,1,128]{2,1,0:T(1,128)S(1)}, u32[]{:S(2)}, u32[]{:S(2)}) collective-permute-start(f32[66,1,128]{2,1,0:T(1,128)S(1)} %get-tuple-element.19), channel_id=1, source_target_pairs={{1,0},{2,1},{3,2},{4,3},{5,4},{6,5},{7,6},{9,8},{10,9},{11,10},{12... | collective-permute-start | bytes 101384 | tf_op jit(solution)/shard_map/ppermute | solution.py:18
  18.1 9.2 %collective-permute-start.7 = (f32[66,1,128]{2,1,0:T(1,128)S(1)}, f32[66,1,128]{2,1,0:T(1,128)S(1)}, u32[]{:S(2)}, u32[]{:S(2)}) collective-permute-start(f32[66,1,128]{2,1,0:T(1,128)S(1)} %get-tuple-element.20), channel_id=1, source_target_pairs={{0,1},{1,2},{2,3},{3,4},{4,5},{5,6},{6,7},{8,9},{9,10},{10,11},{11... | collective-permute-start | bytes 101384 | tf_op jit(solution)/shard_map/ppermute | solution.py:15
  22.7 5.9 %collective-permute-start.6 = (f32[66,1,128]{2,1,0:T(1,128)S(1)}, f32[66,1,128]{2,1,0:T(1,128)S(1)}, u32[]{:S(2)}, u32[]{:S(2)}) collective-permute-start(f32[66,1,128]{2,1,0:T(1,128)S(1)} %slice.194), channel_id=1, source_target_pairs={{0,1},{1,2},{2,3},{3,4},{4,5},{5,6},{6,7},{8,9},{9,10},{10,11},{11... | collective-permute-start | bytes 101384 | tf_op jit(solution)/shard_map/ppermute | solution.py:15
  30.2 24.6 %copy-start.14 = (f32[64,16,128]{2,1,0:T(8,128)}, f32[64,16,128]{2,1,0:T(8,128)S(1)}, u32[]{:S(2)}) copy-start(f32[64,16,128]{2,1,0:T(8,128)S(1)} %get-tuple-element.10) | copy-start | bytes 1572868
  31.5 32.3 %copy-start = (f32[8,64,16,128]{3,0,2,1:T(8,128)}, f32[8,64,16,128]{3,0,2,1:T(8,128)S(1)}, u32[]{:S(2)}) copy-start(f32[8,64,16,128]{3,0,2,1:T(8,128)S(1)} %broadcast_multiply_fusion) | copy-start | bytes 12582916
  31.5 23.3 %copy-start.12 = (f32[64,16,128]{2,1,0:T(8,128)S(1)}, f32[64,16,128]{2,1,0:T(8,128)}, u32[]{:S(2)}) copy-start(f32[64,16,128]{2,1,0:T(8,128)} %param.9) | copy-start | bytes 1572868
  31.5 4.5 %collective-permute-start.8 = (f32[8,1,16,128]{3,0,2,1:T(8,128)S(1)}, f32[8,1,16,128]{3,0,2,1:T(8,128)S(1)}, u32[]{:S(2)}, u32[]{:S(2)}) collective-permute-start(f32[8,1,16,128]{3,0,2,1:T(8,128)S(1)} %get-tuple-element.18), channel_id=1, source_target_pairs={{8,0},{16,8},{24,16},{9,1},{17,9},{25,17},{10,2},{18,10},{26,18},{... | collective-permute-start | bytes 196616 | tf_op jit(solution)/shard_map/ppermute | solution.py:18
  33.0 3.9 %collective-permute-start.9 = (f32[8,1,16,128]{3,0,2,1:T(8,128)S(1)}, f32[8,1,16,128]{3,0,2,1:T(8,128)S(1)}, u32[]{:S(2)}, u32[]{:S(2)}) collective-permute-start(f32[8,1,16,128]{3,0,2,1:T(8,128)S(1)} %get-tuple-element.17), channel_id=1, source_target_pairs={{0,8},{8,16},{16,24},{1,9},{9,17},{17,25},{2,10},{10,18},{18,26},{... | collective-permute-start | bytes 196616 | tf_op jit(solution)/shard_map/ppermute | solution.py:15
  36.9 10.6 %collective-permute-start.10 = (f32[8,66,1,128]{3,0,2,1:T(8,128)S(1)}, f32[8,66,1,128]{3,0,2,1:T(8,128)S(1)}, u32[]{:S(2)}, u32[]{:S(2)}) collective-permute-start(f32[8,66,1,128]{3,0,2,1:T(8,128)S(1)} %get-tuple-element.13), channel_id=1, source_target_pairs={{1,0},{2,1},{3,2},{4,3},{5,4},{6,5},{7,6},{9,8},{10,9},{11,10},{12... | collective-permute-start | bytes 811016 | tf_op jit(solution)/shard_map/ppermute | solution.py:18
  38.2 16.6 %collective-permute-start.11 = (f32[8,66,1,128]{3,0,2,1:T(8,128)S(1)}, f32[8,66,1,128]{3,0,2,1:T(8,128)S(1)}, u32[]{:S(2)}, u32[]{:S(2)}) collective-permute-start(f32[8,66,1,128]{3,0,2,1:T(8,128)S(1)} %get-tuple-element.14), channel_id=1, source_target_pairs={{0,1},{1,2},{2,3},{3,4},{4,5},{5,6},{6,7},{8,9},{9,10},{10,11},{11... | collective-permute-start | bytes 811016 | tf_op jit(solution)/shard_map/ppermute | solution.py:15
  75.2 76.2 %collective-permute-start.12 = (f32[8,1,16,128]{3,0,2,1:T(8,128)}, f32[8,1,16,128]{3,0,2,1:T(8,128)S(1)}, u32[]{:S(2)}, u32[]{:S(2)}) collective-permute-start(f32[8,1,16,128]{3,0,2,1:T(8,128)} %get-tuple-element.16), channel_id=1, source_target_pairs={{8,0},{16,8},{24,16},{9,1},{17,9},{25,17},{10,2},{18,10},{26,18},{... | collective-permute-start | bytes 196616 | tf_op jit(solution)/shard_map/ppermute | solution.py:18
  76.5 74.8 %collective-permute-start.13 = (f32[8,1,16,128]{3,0,2,1:T(8,128)}, f32[8,1,16,128]{3,0,2,1:T(8,128)S(1)}, u32[]{:S(2)}, u32[]{:S(2)}) collective-permute-start(f32[8,1,16,128]{3,0,2,1:T(8,128)} %get-tuple-element.15), channel_id=1, source_target_pairs={{0,8},{8,16},{16,24},{1,9},{9,17},{17,25},{2,10},{10,18},{18,26},{... | collective-permute-start | bytes 196616 | tf_op jit(solution)/shard_map/ppermute | solution.py:15
  152.6 8.5 %collective-permute-start.14 = (f32[8,66,1,128]{3,0,2,1:T(8,128)S(1)}, f32[8,66,1,128]{3,0,2,1:T(8,128)S(1)}, u32[]{:S(2)}, u32[]{:S(2)}) collective-permute-start(f32[8,66,1,128]{3,0,2,1:T(8,128)S(1)} %get-tuple-element.11), channel_id=1, source_target_pairs={{1,0},{2,1},{3,2},{4,3},{5,4},{6,5},{7,6},{9,8},{10,9},{11,10},{12... | collective-permute-start | bytes 811016 | tf_op jit(solution)/shard_map/ppermute | solution.py:18
  154.0 8.5 %collective-permute-start.15 = (f32[8,66,1,128]{3,0,2,1:T(8,128)S(1)}, f32[8,66,1,128]{3,0,2,1:T(8,128)S(1)}, u32[]{:S(2)}, u32[]{:S(2)}) collective-permute-start(f32[8,66,1,128]{3,0,2,1:T(8,128)S(1)} %get-tuple-element.12), channel_id=1, source_target_pairs={{0,1},{1,2},{2,3},{3,4},{4,5},{5,6},{6,7},{8,9},{9,10},{10,11},{11... | collective-permute-start | bytes 811016 | tf_op jit(solution)/shard_map/ppermute | solution.py:15
  158.9 13.5 %copy-start.1 = (f32[8,64,16,128]{3,0,2,1:T(8,128)S(1)}, f32[8,64,16,128]{3,0,2,1:T(8,128)}, u32[]{:S(2)}) copy-start(f32[8,64,16,128]{3,0,2,1:T(8,128)} %copy-done) | copy-start | bytes 12582916
  158.9 13.5 %copy-start.6 = (f32[8,64,16,128]{3,0,2,1:T(8,128)S(1)}, f32[8,64,16,128]{3,0,2,1:T(8,128)}, u32[]{:S(2)}) copy-start(f32[8,64,16,128]{3,0,2,1:T(8,128)} %get-tuple-element.8) | copy-start | bytes 12582916
  (8 other events, 71.4 us)
